TPU v7x, 32 devices: a whole 2x2x4 slice. The times are simulated.
32 devices in a mesh: groups: 2 (over y), expert: 8 (over z, core), attn: 2 (over x).
Axes of the slice: x: 2, y: 2, z: 4, core: 2. Of those that a mesh axis runs over, the one named last changes fastest.
Arguments:
- tokens: bfloat16 [512, 3584], P(('groups', 'expert')), parts along dimension 0, may hold values from -6 to 6
- gates: float32 [512, 8], P(('groups', 'expert')), parts along dimension 0, may hold values from 0.05 to 0.6
- slots: int32 [512, 8], P(('groups', 'expert')), parts along dimension 0, may hold values from 0 to 15, all different within a row; in each aligned block of 32 rows (0 to 31, 32 to 63, ...) at most 20 rows name the same one
- plan: int32 [16], P('groups'), parts along dimension 0, may hold values from 0 to 7, as said below
- gate_proj: bfloat16 [8, 3584, 1024], P('expert', None, 'attn'), may hold values from -0.09375 to 0.09375
- up_proj: bfloat16 [8, 3584, 1024], P('expert', None, 'attn'), may hold values from -0.09375 to 0.09375
- down_proj: bfloat16 [8, 3584, 1024], P('expert', None, 'attn'), may hold values from -0.1875 to 0.1875
Outputs:
- moe_out: bfloat16 [512, 3584], P(('groups', 'expert')), parts along dimension 0
There are 2 independent parts, one for each index of `groups`. A program takes and returns all parts, laid end to end along the dimension named above; an argument that names none is the same for every part. Nothing has to cross between parts.
Inputs may be any that keep to these rules, and one draw needn't show every extreme that they name: A row's 8 slots are distinct; among the 32 rows of one index of expert (aligned blocks) no slot is named more than 20 times, a bound that some block reaches. plan[d] is never d; no expert is named by more than 2 entries of plan, and some expert by exactly 2.
All inputs are finite; a program needn't handle non-finite values.
Results may differ from a plain program's by a relative error of at most 0.014.
Values may be sent and summed in bfloat16 or wider, within the bound.
A program may use at most 128 MiB of HBM per device.

v0:
```python
import jax
import jax.numpy as jnp
from jax import lax
from jax.sharding import PartitionSpec as P

MULT = 2


def expert_rows(rows, w_gate, w_up, w_down):
    gate_act = jnp.dot(rows, w_gate, preferred_element_type=jnp.float32)
    up_act = jnp.dot(rows, w_up, preferred_element_type=jnp.float32)
    hidden = (jax.nn.silu(gate_act) * up_act).astype(jnp.bfloat16)
    down_out = jnp.einsum("rf,df->rd", hidden, w_down, preferred_element_type=jnp.float32)
    return down_out.astype(jnp.bfloat16)


def slot_ranks(slot_keys, key_count):
    onehot = (slot_keys[:, None] == jnp.arange(key_count, dtype=jnp.int32)[None, :]).astype(
        jnp.int32
    )
    return jnp.sum(jnp.cumsum(onehot, axis=0) * onehot, axis=1) - 1


def spread_rows(row_index, row_total, tok_count, top_count):
    matches = (
        row_index.reshape(tok_count, top_count)[None, :, :]
        == jnp.arange(row_total, dtype=jnp.int32)[:, None, None]
    )
    return jnp.sum(matches.astype(jnp.int32), axis=2).astype(jnp.bfloat16)


def body(tokens, gates, slots, plan, gate_proj, up_proj, down_proj):
    experts = lax.axis_size("expert")
    tok_count, model_width = tokens.shape
    top_count = slots.shape[1]
    capacity = max(2, min(tok_count, tok_count * top_count * 5 // (8 * experts)))
    flat_slots = slots.reshape(-1)
    device = flat_slots // 2
    slot_kind = flat_slots % 2
    owner_device = jnp.where(slot_kind == 0, device, plan[device])
    per_owner = (1 + MULT) * capacity
    position = slot_ranks(owner_device, experts)
    row_index = owner_device * per_owner + position
    row_total = experts * per_owner
    dispatch = spread_rows(row_index, row_total, tok_count, top_count)
    outgoing = jnp.dot(dispatch, tokens, preferred_element_type=jnp.float32).astype(jnp.bfloat16)
    outgoing = outgoing.reshape(experts, per_owner, model_width)
    incoming = lax.all_to_all(outgoing, "expert", split_axis=0, concat_axis=0, tiled=True)
    results = expert_rows(
        incoming.reshape(row_total, model_width), gate_proj[0], up_proj[0], down_proj[0]
    )
    results = results.reshape(experts, per_owner, model_width)
    returned = lax.all_to_all(results, "expert", split_axis=0, concat_axis=0, tiled=True).reshape(
        row_total, model_width
    )
    choice_rows = row_index.reshape(tok_count, top_count)
    partial_value = jnp.zeros((tok_count, returned.shape[1]), jnp.float32)
    for column in range(top_count):
        partial_value = (
            partial_value
            + returned[choice_rows[:, column]].astype(jnp.float32) * gates[:, column][:, None]
        )
    return lax.psum(partial_value.astype(jnp.bfloat16), "attn")


def solution(mesh):
    return jax.shard_map(
        body,
        mesh=mesh,
        in_specs=(
            P(("groups", "expert"), None),
            P(("groups", "expert"), None),
            P(("groups", "expert"), None),
            P("groups"),
            P("expert", None, "attn"),
            P("expert", None, "attn"),
            P("expert", None, "attn"),
        ),
        out_specs=P(("groups", "expert"), None),
        check_vma=False,
    )
```

profile of v0, /device:TPU:0, one launch (start us, length us, event | category | flops | bytes accessed | tf_op | source)
XLA Modules:
  0.0 286.4 jit_solution(9104749936648108147)
XLA Ops:
  6.5 0.8 copy.23
  7.3 0.1 reshape.197
  7.6 1.6 fusion.32
  9.2 4.3 %compare_select_fusion.9 = (s32[256,1]{0,1:T(1,128)S(1)}, s32[256,1]{0,1:T(1,128)S(1)}) fusion(s32[]{:T(128)} %bitcast.1, s32[]{:T(128)} %bitcast.2, s32[]{:T(128)} %bitcast.3, s32[]{:T(128)} %bitcast.4, s32[]{:T(128)} %bitcast.5, s32[]{:T(128)} %bitcast.7, s32[]{:T(128)} %bitcast.6, s32[256,1]{0,1:T(1,128)S(1)} %reshape.197), kind=kLoop, calls=%fused_computation.66 | loop fusion | flops 7680 | bytes 3100 | tf_op jit(solution)/shard_map/gather | solution.py:40
  13.6 0.7 compare_select_fusion.19
  14.3 0.6 reduce-window.6
  14.9 0.2 slice_reduce_fusion
  15.2 0.1 fusion.29
  15.4 0.2 convert_reduce_fusion
  15.7 2.9 convolution_convert_fusion.1
  18.5 4.6 %reshape.201 = bf16[8,60,3584]{2,1,0:T(8,128)(2,1)} reshape(bf16[480,3584]{1,0:T(8,128)(2,1)} %convolution_convert_fusion.1) | data formatting | bytes 6881280 | tf_op jit(solution)/shard_map/reshape | solution.py:47
  23.1 89.2 %all_to_all.10 = bf16[8,60,3584]{2,1,0:T(8,128)(2,1)} all-to-all(bf16[8,60,3584]{2,1,0:T(8,128)(2,1)} %reshape.201), channel_id=1, replica_groups=mesh['groups'=2,'expert'=8,'attn'=2] {'expert'}, dimensions={0} | all-to-all | bytes 6881280 | tf_op jit(solution)/shard_map/all_to_all | solution.py:48
  112.3 4.6 %reshape.202 = bf16[480,3584]{1,0:T(8,128)(2,1)} reshape(bf16[8,60,3584]{2,1,0:T(8,128)(2,1)} %all_to_all.10) | data formatting | bytes 6881280 | tf_op jit(solution)/shard_map/reshape | solution.py:50
  116.9 5.0 %fusion.3 = f32[480,512]{1,0:T(8,128)S(1)} fusion(bf16[480,3584]{1,0:T(8,128)(2,1)} %reshape.202, bf16[1,3584,512]{2,1,0:T(8,128)(2,1)} %param.11), kind=kOutput, calls=%fused_computation.13 | convolution fusion | flops 1761607680 | bytes 8093696 | tf_op jit(solution)/shard_map/dot_general | solution.py:10
  121.9 9.7 %convolution_convert_fusion = bf16[480,3584]{1,0:T(8,128)(2,1)} fusion(bf16[1,3584,512]{2,1,0:T(8,128)(2,1)} %param.13, bf16[480,3584]{1,0:T(8,128)(2,1)} %reshape.202, bf16[1,3584,512]{2,1,0:T(8,128)(2,1)} %param.12, f32[480,512]{1,0:T(8,128)S(1)} %fusion.3), kind=kOutput, calls=%fused_computation.8 | convolution fusion | flops 3526410240 | bytes 15204352 | tf_op jit(solution)/shard_map/rf,df->rd/dot_general | solution.py:13
  131.7 4.6 %reshape.203 = bf16[8,60,3584]{2,1,0:T(8,128)(2,1)} reshape(bf16[480,3584]{1,0:T(8,128)(2,1)} %convolution_convert_fusion) | data formatting | bytes 6881280 | tf_op jit(solution)/shard_map/reshape | solution.py:52
  136.3 4.6 %all-to-all-start.1 = ((bf16[8,60,3584]{2,1,0:T(8,128)(2,1)}), bf16[8,60,3584]{2,1,0:T(8,128)(2,1)}, u32[]{:S(2)}, u32[]{:S(2)}) async-start(bf16[8,60,3584]{2,1,0:T(8,128)(2,1)} %reshape.203), calls=%async_computation.1 | async-start | bytes 7340032 | tf_op jit(solution)/shard_map/all_to_all | solution.py:53
  140.9 0.2 all-reduce.2.cloned.1.call-start
  141.2 0.3 fusion.19
  141.6 82.1 %all-to-all-done.1 = bf16[8,60,3584]{2,1,0:T(8,128)(2,1)} async-done(((bf16[8,60,3584]{2,1,0:T(8,128)(2,1)}), bf16[8,60,3584]{2,1,0:T(8,128)(2,1)}, u32[]{:S(2)}, u32[]{:S(2)}) %all-to-all-start.1) | async-done | bytes 3440672 | tf_op jit(solution)/shard_map/all_to_all | solution.py:53
  223.7 4.6 %reshape.204 = bf16[480,3584]{1,0:T(8,128)(2,1)} reshape(bf16[8,60,3584]{2,1,0:T(8,128)(2,1)} %all-to-all-done.1) | data formatting | bytes 6881280 | tf_op jit(solution)/shard_map/reshape | solution.py:53
  228.3 3.3 %gather_fusion = bf16[32,3584]{1,0:T(8,128)(2,1)S(1)} fusion(bf16[480,3584]{1,0:T(8,128)(2,1)} %reshape.204, s32[1024]{0:T(1024)S(1)} %get-tuple-element.40), kind=kCustom, calls=%fused_computation | custom fusion | bytes 458880 | tf_op jit(solution)/shard_map/gather | solution.py:61
  231.6 3.3 %gather_fusion.1 = bf16[32,3584]{1,0:T(8,128)(2,1)S(1)} fusion(bf16[480,3584]{1,0:T(8,128)(2,1)} %reshape.204, s32[1024]{0:T(1024)S(1)} %get-tuple-element.39), kind=kCustom, calls=%fused_computation.1 | custom fusion | bytes 458880 | tf_op jit(solution)/shard_map/gather | solution.py:61
  234.9 3.3 %gather_fusion.2 = bf16[32,3584]{1,0:T(8,128)(2,1)S(1)} fusion(bf16[480,3584]{1,0:T(8,128)(2,1)} %reshape.204, s32[1024]{0:T(1024)S(1)} %get-tuple-element.38), kind=kCustom, calls=%fused_computation.2 | custom fusion | bytes 458880 | tf_op jit(solution)/shard_map/gather | solution.py:61
  238.3 3.3 %gather_fusion.3 = bf16[32,3584]{1,0:T(8,128)(2,1)S(1)} fusion(bf16[480,3584]{1,0:T(8,128)(2,1)} %reshape.204, s32[1024]{0:T(1024)S(1)} %get-tuple-element.37), kind=kCustom, calls=%fused_computation.3 | custom fusion | bytes 458880 | tf_op jit(solution)/shard_map/gather | solution.py:61
  241.6 3.3 %gather_fusion.4 = bf16[32,3584]{1,0:T(8,128)(2,1)S(1)} fusion(bf16[480,3584]{1,0:T(8,128)(2,1)} %reshape.204, s32[1024]{0:T(1024)S(1)} %get-tuple-element.36), kind=kCustom, calls=%fused_computation.4 | custom fusion | bytes 458880 | tf_op jit(solution)/shard_map/gather | solution.py:61
  244.9 3.3 %gather_fusion.5 = bf16[32,3584]{1,0:T(8,128)(2,1)S(1)} fusion(bf16[480,3584]{1,0:T(8,128)(2,1)} %reshape.204, s32[1024]{0:T(1024)S(1)} %get-tuple-element.35), kind=kCustom, calls=%fused_computation.5 | custom fusion | bytes 458880 | tf_op jit(solution)/shard_map/gather | solution.py:61
  248.2 3.3 %gather_fusion.6 = bf16[32,3584]{1,0:T(8,128)(2,1)S(1)} fusion(bf16[480,3584]{1,0:T(8,128)(2,1)} %reshape.204, s32[1024]{0:T(1024)S(1)} %get-tuple-element.34), kind=kCustom, calls=%fused_computation.6 | custom fusion | bytes 458880 | tf_op jit(solution)/shard_map/gather | solution.py:61
  251.6 3.3 %gather_fusion.7 = bf16[32,3584]{1,0:T(8,128)(2,1)S(1)} fusion(bf16[480,3584]{1,0:T(8,128)(2,1)} %reshape.204, s32[1024]{0:T(1024)S(1)} %get-tuple-element.33), kind=kCustom, calls=%fused_computation.7 | custom fusion | bytes 458880 | tf_op jit(solution)/shard_map/gather | solution.py:61
  254.9 1.1 add_convert_fusion
  256.0 21.9 %all-reduce.2.cloned.1.call-done = bf16[32,3584]{1,0:T(8,128)(2,1)} async-done(((bf16[32,3584]{1,0:T(8,128)(2,1)}), bf16[32,3584]{1,0:T(8,128)(2,1)}) %all-reduce.2.cloned.1.call-update) | async-done | bytes 229392 | tf_op jit(solution)/shard_map/psum | solution.py:63
  277.9 1.6 copy.31
  (21 shorter events, 0.5 us)
Async XLA Ops:
  6.5 9.1 %copy-start = (bf16[32,3584]{1,0:T(8,128)(2,1)S(1)}, bf16[32,3584]{1,0:T(8,128)(2,1)}, u32[]{:S(2)}) copy-start(bf16[32,3584]{1,0:T(8,128)(2,1)} %param.7) | copy-start | bytes 688132
  136.3 5.2 %copy-start.1 = (f32[32,8]{0,1:T(8,128)S(1)}, f32[32,8]{0,1:T(8,128)}, u32[]{:S(2)}) copy-start(f32[32,8]{0,1:T(8,128)} %param.8) | copy-start | bytes 3076
  136.3 87.4 %all-to-all-start.1 = ((bf16[8,60,3584]{2,1,0:T(8,128)(2,1)}), bf16[8,60,3584]{2,1,0:T(8,128)(2,1)}, u32[]{:S(2)}, u32[]{:S(2)}) async-start(bf16[8,60,3584]{2,1,0:T(8,128)(2,1)} %reshape.203), calls=%async_computation.1 | async-start | bytes 7340032 | tf_op jit(solution)/shard_map/all_to_all | solution.py:53
  140.9 137.0 %all-reduce.2.cloned.1.call-start = ((), (), s32[]{:S(2)}) async-start(), calls=%async_computation.2 | async-start | bytes 458752 | tf_op jit(solution)/shard_map/psum | solution.py:63
Sparse Core Ops, SparseCore 0:
  256.2 21.7 all-reduce.1
where the time goes:
time: 287 us; the launch traced here: 286 us
  waiting for transfers between devices  104 us (36%)
  blocking collectives  89.2 us (31%)
  local copies, waits for them, and re-layouts  49.7 us (17%)
  matrix products  17.6 us (6%)
  between operations  13.6 us (5%)
  other arithmetic  7.44 us (3%)
  starting transfers between devices  4.85 us (2%)
    all_to_all x1, blocking collectives, body(): lax.all_to_all(outgoing, 'expert', split_axis=0, concat_axis=0, tiled=True)  89.2 us
    all_to_all x1, waiting for transfers between devices, body(): lax.all_to_all(results, 'expert', split_axis=0, concat_axis=0, tiled=True)  82.1 us
    gather x8, local copies, waits for them, and re-layouts, body(): returned[choice_rows[:, column]].astype(jnp.float32)  26.6 us
    psum x1, waiting for transfers between devices, body(): return lax.psum(partial_value.astype(jnp.bfloat16), 'attn')  21.9 us
    dot_general x1, matrix products, expert_rows(): jnp.einsum('rf,df->rd', hidden, w_down, preferred_element_type=jnp.float32)  9.75 us
  transfers between devices with their start and end apart: 2, of which 2 were waited for; matrix products, arithmetic and copies ran while one was open for 0% of the time, Pallas kernels for 0%

commit v1 on v0

v1 whole, which is shorter than its diff:
```python
import functools

import jax
import jax.numpy as jnp
from jax import lax
from jax.experimental import pallas as pl
from jax.experimental.pallas import tpu as pltpu
from jax.sharding import PartitionSpec as P

MESH = pl.DeviceIdType.MESH
LANES = 128
LAG = 3


def combined_gates(gates, slots, plan, experts):
    choice = slots // 2
    expert = jnp.where(slots % 2 == 0, choice, plan[choice])
    ids = jnp.arange(experts, dtype=jnp.int32)
    return jnp.sum(jnp.where(expert[:, :, None] == ids, gates[:, :, None], 0.0), axis=1)


def dense_body(tokens, gates, slots, plan, gate_proj, up_proj, down_proj):
    experts = lax.axis_size("expert")
    weight = combined_gates(gates, slots, plan, experts)
    everyone = lax.all_gather(tokens, "expert", axis=0, tiled=True)
    weights = lax.all_to_all(weight, "expert", split_axis=1, concat_axis=0, tiled=True)
    gate_act = jnp.dot(everyone, gate_proj[0], preferred_element_type=jnp.float32)
    up_act = jnp.dot(everyone, up_proj[0], preferred_element_type=jnp.float32)
    hidden = (jax.nn.silu(gate_act) * up_act).astype(jnp.bfloat16)
    down = jnp.einsum("rf,df->rd", hidden, down_proj[0], preferred_element_type=jnp.float32)
    part = (down * weights).astype(jnp.bfloat16)
    part = lax.psum_scatter(part, "expert", scatter_dimension=0, tiled=True)
    return lax.psum(part, "attn")


def kernel(
    nz, steps, width,
    tokens, gates, slots, plan, gate_hbm, up_hbm, down_hbm,
    out,
    rows, wg, wu, wd, hid, scale, grow_send, grow,
    keep, a_send, a_recv, b_send, b_recv, c_send, c_recv, d_send,
    send_sem, local_sem, row_sem, g_sem, a_sem, b_sem, c_sem, d_sem,
):
    f32, bf16 = jnp.float32, jnp.bfloat16
    experts = 2 * nz
    me = lax.axis_index("expert")
    x = lax.axis_index("attn")
    z, c = me // 2, me % 2
    half = rows.shape[-1]
    tok = rows.shape[-2]
    mine = pl.ds(pl.multiple_of(x * half, LANES), half)
    other = pl.ds(pl.multiple_of((1 - x) * half, LANES), half)
    partner = {"expert": z * 2 + (1 - c)}
    across = {"attn": 1 - x}

    counts = {"send": 0, "local": 0}
    pending = []

    def local(src, dst):
        copy = pltpu.make_async_copy(src, dst, local_sem.at[counts["local"]])
        counts["local"] += 1
        copy.start()
        return copy

    def send(src, dst, sem, device, when=None):
        copy = pltpu.make_async_remote_copy(
            src_ref=src, dst_ref=dst, send_sem=send_sem.at[counts["send"]], recv_sem=sem,
            device_id=device, device_id_type=MESH,
        )
        counts["send"] += 1
        if when is None:
            copy.start()
        else:
            pl.when(when)(copy.start)
        pending.append((when, copy))

    def arrived(dst, sem):
        pltpu.make_async_remote_copy(
            src_ref=dst, dst_ref=dst, send_sem=send_sem.at[0], recv_sem=sem,
            device_id=partner, device_id_type=MESH,
        ).wait_recv()

    own_copies = [
        local(tokens.at[:, mine], rows.at[0, 0, z]),
        local(tokens.at[:, other], rows.at[1, 0, z]),
    ]
    weight_copies = []
    for h, part in enumerate((mine, other)):
        weight_copies.append(local(gate_hbm.at[0, part, :], wg.at[h]))
        weight_copies.append(local(up_hbm.at[0, part, :], wu.at[h]))
    down_copies = [local(down_hbm.at[0, other, :], wd.at[1]), local(down_hbm.at[0, mine, :], wd.at[0])]

    barrier = pltpu.get_barrier_semaphore()
    for dz in range(nz):
        for r in range(2):
            if dz or r:
                peer = {"expert": ((z + dz) % nz) * 2 + (c if r == 0 else 1 - c)}
                pl.semaphore_signal(barrier, inc=1, device_id=peer, device_id_type=MESH)
    pl.semaphore_signal(barrier, inc=1, device_id=across, device_id_type=MESH)

    diagonal = lax.broadcasted_iota(jnp.int32, (tok, LANES), 0) == lax.broadcasted_iota(
        jnp.int32, (tok, LANES), 1
    )
    named = slots[...]
    expert = lax.shift_right_logical(named, 1)
    target = expert
    for d in range(experts):
        target = jnp.where(expert == d, plan[d], target)
    expert = jnp.where((named & 1) == 0, expert, target)
    gate = gates[...]
    for e in range(experts):
        column = jnp.sum(jnp.where(expert == e, gate, 0.0), axis=1, keepdims=True)
        grow_send[e] = jnp.sum(jnp.where(diagonal, column, 0.0), axis=0, keepdims=True)

    pl.semaphore_wait(barrier, experts)

    for step in (1, -1):
        send(
            tokens.at[:, mine], rows.at[0, 0, z], row_sem.at[0, 0, z],
            {"expert": (z + step) * 2 + c}, (z + step >= 0) & (z + step < nz),
        )
    send(tokens.at[:, mine], rows.at[0, 1, z], row_sem.at[0, 1, z], partner)
    send(tokens.at[:, other], rows.at[1, 1, z], row_sem.at[1, 1, z], partner)
    for dz in range(nz):
        for r in range(2):
            if dz or r:
                peer = ((z + dz) % nz) * 2 + (c if r == 0 else 1 - c)
                send(grow_send.at[peer], grow.at[r, z], g_sem.at[r, z], {"expert": peer})
    grow[0, z] = grow_send[me]

    for hop in range(1, nz + 1):
        for step in (1, -1):
            if hop < nz:
                origin = z - step * hop
                valid = (origin >= 0) & (origin < nz)
                slot = jnp.clip(origin, 0, nz - 1)
                block = rows.at[0, 0, slot]
                pl.when(valid)(functools.partial(arrived, block, row_sem.at[0, 0, slot]))
                if hop < nz - 1:
                    send(
                        block, block, row_sem.at[0, 0, slot], {"expert": (z + step) * 2 + c},
                        valid & (z + step >= 0) & (z + step < nz),
                    )
                send(block, rows.at[1, 0, slot], row_sem.at[1, 0, slot], across, valid)
                send(block, rows.at[0, 1, slot], row_sem.at[0, 1, slot], partner, valid)
        for step in (1, -1):
            if hop > 1:
                origin = z - step * (hop - 1)
                valid = (origin >= 0) & (origin < nz)
                slot = jnp.clip(origin, 0, nz - 1)
                block = rows.at[1, 0, slot]
                pl.when(valid)(functools.partial(arrived, block, row_sem.at[1, 0, slot]))
                send(block, rows.at[1, 1, slot], row_sem.at[1, 1, slot], partner, valid)

    for dz in range(nz):
        for r in range(2):
            if dz or r:
                slot = (z + dz) % nz
                arrived(grow.at[r, slot], g_sem.at[r, slot])
    for r in range(2):
        for i in range(nz):
            column = jnp.sum(jnp.where(diagonal, grow[r, i], 0.0), axis=1, keepdims=True)
            scale[r, i] = jnp.broadcast_to(column, (tok, width))
    for copy in own_copies + weight_copies:
        copy.wait()
    for dz in range(nz):
        slot = (z + dz) % nz
        for h in range(2):
            arrived(rows.at[h, 1, slot], row_sem.at[h, 1, slot])

    total = 2 * nz * tok
    units = wg.shape[-1]
    tile = 256 if units % 256 == 0 else LANES
    for t in range(units // tile):
        cols = pl.ds(t * tile, tile)
        gate_act = up_act = None
        for h in range(2):
            block = rows[h].reshape(total, half)
            g = jnp.dot(block, wg[h, :, cols], preferred_element_type=f32)
            u = jnp.dot(block, wu[h, :, cols], preferred_element_type=f32)
            gate_act = g if gate_act is None else gate_act + g
            up_act = u if up_act is None else up_act + u
        hid[:, cols] = (gate_act / (1.0 + jnp.exp(-gate_act)) * up_act).astype(bf16)

    for copy in down_copies:
        copy.wait()

    def cross(j):
        arrived(a_recv.at[1, j], a_sem.at[1, j])
        b_send[j] = (keep[1, j] + a_recv[1, j].astype(f32)).astype(bf16)
        send(b_send.at[j], b_recv.at[j], b_sem.at[j], across)

    for j in range(steps):
        for h in (1, 0):
            down = lax.dot_general(
                hid[...], wd[h, pl.ds(j * width, width), :], (((1,), (1,)), ((), ())),
                preferred_element_type=f32,
            )
            down = down.reshape(2, nz, tok, width) * scale[...]
            a_send[h, j] = down[1].astype(bf16)
            keep[h, j] = down[0]
            send(a_send.at[h, j], a_recv.at[h, j], a_sem.at[h, j], partner)
        if j:
            cross(j - 1)
    cross(steps - 1)

    out_copies = []

    def finish(j):
        value = keep[0, j, z] + a_recv[0, j, z].astype(f32) + b_recv[j, z].astype(f32)
        for d in range(nz - 1):
            arrived(c_recv.at[j, d], c_sem.at[j, d])
        for d in range(nz - 1):
            value = value + c_recv[j, d].astype(f32)
        d_send[j] = value.astype(bf16)
        cols = pl.ds(pl.multiple_of(x * half + j * width, LANES), width)
        send(d_send.at[j], out.at[:, cols], d_sem.at[j], across)
        out_copies.append(local(d_send.at[j], out.at[:, cols]))

    for j in range(steps + LAG):
        if j < steps:
            arrived(a_recv.at[0, j], a_sem.at[0, j])
            arrived(b_recv.at[j], b_sem.at[j])
            c_send[j] = (keep[0, j] + a_recv[0, j].astype(f32) + b_recv[j].astype(f32)).astype(bf16)
            for d in range(nz - 1):
                peer = (z + d + 1) % nz
                send(
                    c_send.at[j, peer], c_recv.at[j, d], c_sem.at[j, d], {"expert": peer * 2 + c}
                )
        if j >= LAG:
            finish(j - LAG)

    for j in range(steps):
        cols = pl.ds(pl.multiple_of((1 - x) * half + j * width, LANES), width)
        arrived(out.at[:, cols], d_sem.at[j])
    for copy in out_copies:
        copy.wait()
    for when, copy in pending:
        if when is None:
            copy.wait_send()
        else:
            pl.when(when)(copy.wait_send)


def fused_body(tokens, gates, slots, plan, gate_proj, up_proj, down_proj):
    f32, bf16 = jnp.float32, jnp.bfloat16
    nz = lax.axis_size("expert") // 2
    tok, model = tokens.shape
    half = model // 2
    units = gate_proj.shape[2]
    width = 256 if half % 256 == 0 else LANES
    steps = half // width
    dma = pltpu.SemaphoreType.DMA
    vmem, anywhere = pl.BlockSpec(memory_space=pltpu.VMEM), pl.BlockSpec(memory_space=pl.ANY)
    sends = 4 + 2 * nz + 8 * nz + steps * (3 + nz) + 4
    return pl.pallas_call(
        functools.partial(kernel, nz, steps, width),
        out_shape=jax.ShapeDtypeStruct((tok, model), bf16),
        in_specs=[
            anywhere, vmem, vmem, pl.BlockSpec(memory_space=pltpu.SMEM),
            anywhere, anywhere, anywhere,
        ],
        out_specs=anywhere,
        scratch_shapes=[
            pltpu.VMEM((2, 2, nz, tok, half), bf16),
            pltpu.VMEM((2, half, units), bf16),
            pltpu.VMEM((2, half, units), bf16),
            pltpu.VMEM((2, half, units), bf16),
            pltpu.VMEM((2 * nz * tok, units), bf16),
            pltpu.VMEM((2, nz, tok, width), f32),
            pltpu.VMEM((2 * nz, 1, LANES), f32),
            pltpu.VMEM((2, nz, 1, LANES), f32),
            pltpu.VMEM((2, steps, nz, tok, width), f32),
            pltpu.VMEM((2, steps, nz, tok, width), bf16),
            pltpu.VMEM((2, steps, nz, tok, width), bf16),
            pltpu.VMEM((steps, nz, tok, width), bf16),
            pltpu.VMEM((steps, nz, tok, width), bf16),
            pltpu.VMEM((steps, nz, tok, width), bf16),
            pltpu.VMEM((steps, nz - 1, tok, width), bf16),
            pltpu.VMEM((steps, tok, width), bf16),
            dma((sends,)),
            dma((8 + steps,)),
            dma((2, 2, nz)),
            dma((2, nz)),
            dma((2, steps)),
            dma((steps,)),
            dma((steps, nz - 1)),
            dma((steps,)),
        ],
        compiler_params=pltpu.CompilerParams(
            collective_id=0, has_side_effects=True, vmem_limit_bytes=48 * 1024 * 1024
        ),
    )(tokens, gates, slots, plan, gate_proj, up_proj, down_proj)


def body(tokens, gates, slots, plan, gate_proj, up_proj, down_proj):
    experts, attn = lax.axis_size("expert"), lax.axis_size("attn")
    tok, model = tokens.shape
    fits = (
        attn == 2 and experts % 2 == 0 and experts > 2
        and tok % 16 == 0 and tok <= LANES
        and model % (2 * LANES) == 0 and gate_proj.shape[0] == 1
        and gate_proj.shape[2] % LANES == 0
    )
    chosen = fused_body if fits else dense_body
    return chosen(tokens, gates, slots, plan, gate_proj, up_proj, down_proj)


def solution(mesh):
    return jax.shard_map(
        body,
        mesh=mesh,
        in_specs=(
            P(("groups", "expert"), None),
            P(("groups", "expert"), None),
            P(("groups", "expert"), None),
            P("groups"),
            P("expert", None, "attn"),
            P("expert", None, "attn"),
            P("expert", None, "attn"),
        ),
        out_specs=P(("groups", "expert"), None),
        check_vma=False,
    )
```

time: 287 us -> 53.5 us (0.19)
  waiting for transfers between devices: 104 us -> 0 us
  blocking collectives: 89.2 us -> 0 us
  Pallas kernels: 0 us -> 47.4 us
  local copies, waits for them, and re-layouts: 49.7 us -> 5.84 us
  matrix products: 17.6 us -> 0 us
  between operations: 13.6 us -> 0.01 us
  other arithmetic: 7.44 us -> 0 us
  starting transfers between devices: 4.85 us -> 0 us
    all_to_all x1 -> x0, blocking collectives: 89.2 us -> none  [body(): lax.all_to_all(outgoing, 'expert', split_axis=0, concat_axis=0, tiled=True)]
    all_to_all x1 -> x0, waiting for transfers between devices: 82.1 us -> none  [body(): lax.all_to_all(results, 'expert', split_axis=0, concat_axis=0, tiled=True)]
    pallas_call x0 -> x1, Pallas kernels: none -> 47.4 us  [fused_body(): pl.pallas_call(functools.partial(kernel, nz, steps, width), out_shape=jax...]
    gather x10 -> x0, local copies, waits for them, and re-layouts: 28.3 us -> none  [the longest x8 26.6 us: body(): returned[choice_rows[:, column]].astype(jnp.float32)]
    psum x1 -> x0, waiting for transfers between devices: 21.9 us -> none  [body(): return lax.psum(partial_value.astype(jnp.bfloat16), 'attn')]
    reshape x7 -> x0, local copies, waits for them, and re-layouts: 18.7 us -> none  [the longest x1 4.62 us: body(): results = results.reshape(experts, per_owner, model_width)]
    dot_general x3 -> x0, matrix products: 17.6 us -> none  [the longest x1 9.75 us: expert_rows(): jnp.einsum('rf,df->rd', hidden, w_down, preferred_element_type=jnp.float32)]
    all_to_all x1 -> x0, starting transfers between devices: 4.63 us -> none  [body(): lax.all_to_all(results, 'expert', split_axis=0, concat_axis=0, tiled=True)]
  transfers between devices with their start and end apart: 2 -> 0, of which waited for: 2 -> 0; matrix products, arithmetic and copies ran while one was open for 0% -> 0% of each run, Pallas kernels for 0% -> 0%
where the time goes in v1:
time: 53.5 us; the launch traced here: 53.2 us
  Pallas kernels  47.4 us (89%)
  local copies, waits for them, and re-layouts  5.84 us (11%)
    pallas_call x1, Pallas kernels, fused_body(): pl.pallas_call(functools.partial(kernel, nz, steps, width), out_shape=jax...  47.4 us
    unnamed x9, local copies, waits for them, and re-layouts  5.84 us

profile of v1, /device:TPU:0, one launch (start us, length us, event | category | flops | bytes accessed | tf_op | source)
XLA Modules:
  0.0 53.2 jit_solution(13573083127051225013)
XLA Ops:
  0.0 0.8 %copy.8.gates = f32[32,8]{1,0:T(8,128)S(1)} copy(f32[32,8]{0,1:T(8,128)} %param.8) | data formatting | bytes 2048 | tf_op args[1]
  0.8 0.8 %copy.9.slots = s32[32,8]{1,0:T(8,128)S(1)} copy(s32[32,8]{0,1:T(8,128)} %param.9) | data formatting | bytes 2048 | tf_op args[2]
  1.5 0.0 copy-start
  1.5 2.0 %copy-done = bf16[1,3584,512]{2,1,0:T(8,128)(2,1)S(1)} copy-done((bf16[1,3584,512]{2,1,0:T(8,128)(2,1)S(1)}, bf16[1,3584,512]{2,1,0:T(8,128)(2,1)}, u32[]{:S(2)}) %copy-start) | copy-done | bytes 3670040
  3.6 0.0 copy-start.1
  3.6 0.9 %copy-done.1 = bf16[32,3584]{1,0:T(8,128)(2,1)S(1)} copy-done((bf16[32,3584]{1,0:T(8,128)(2,1)S(1)}, bf16[32,3584]{1,0:T(8,128)(2,1)}, u32[]{:S(2)}) %copy-start.1) | copy-done | bytes 229400
  4.5 0.0 copy-start.2
  4.5 0.7 %copy-done.2 = s32[8]{0:T(128)S(1)} copy-done((s32[8]{0:T(128)S(1)}, s32[8]{0:T(128)}, u32[]{:S(2)}) %copy-start.2) | copy-done | bytes 56
  5.2 47.4 %shard_map.73 = bf16[32,3584]{1,0:T(8,128)(2,1)S(1)} custom-call(bf16[32,3584]{1,0:T(8,128)(2,1)S(1)} %copy-done.1, f32[32,8]{1,0:T(8,128)S(1)} %copy.8.gates, s32[32,8]{1,0:T(8,128)S(1)} %copy.9.slots, s32[8]{0:T(128)S(1)} %copy-done.2, bf16[1,3584,512]{2,1,0:T(8,128)(2,1)S(1)} %copy-done, bf16[1,3584,512]{2,1,0:T(8,128)(2,1)} %up_hbm.1, ...), custom_call_target="tpu_custom_call" | custom-call | tf_op jit(solution)/shard_map/pallas_call | solution.py:256
  52.5 0.7 %copy.11 = bf16[32,3584]{1,0:T(8,128)(2,1)} copy(bf16[32,3584]{1,0:T(8,128)(2,1)S(1)} %shard_map.73) | data formatting | bytes 458752
Async XLA Ops:
  1.5 2.0 %copy-start = (bf16[1,3584,512]{2,1,0:T(8,128)(2,1)S(1)}, bf16[1,3584,512]{2,1,0:T(8,128)(2,1)}, u32[]{:S(2)}) copy-start(bf16[1,3584,512]{2,1,0:T(8,128)(2,1)} %gate_hbm.1) | copy-start | bytes 11010052
  3.6 0.9 %copy-start.1 = (bf16[32,3584]{1,0:T(8,128)(2,1)S(1)}, bf16[32,3584]{1,0:T(8,128)(2,1)}, u32[]{:S(2)}) copy-start(bf16[32,3584]{1,0:T(8,128)(2,1)} %tokens.1) | copy-start | bytes 688132
  4.5 0.7 %copy-start.2 = (s32[8]{0:T(128)S(1)}, s32[8]{0:T(128)}, u32[]{:S(2)}) copy-start(s32[8]{0:T(128)} %plan.1) | copy-start | bytes 100

commit v2 on v1

--- a/solution.py
+++ b/solution.py
@@ -10,6 +10,7 @@
 MESH = pl.DeviceIdType.MESH
 LANES = 128
 LAG = 3
+ROWS = 16
 
 
 def combined_gates(gates, slots, plan, experts):
@@ -37,7 +38,7 @@
     nz, steps, width,
     tokens, gates, slots, plan, gate_hbm, up_hbm, down_hbm,
     out,
-    rows, wg, wu, wd, hid, scale, grow_send, grow,
+    rows, wg, wu, wd, acc, hid, scale, grow_send, grow,
     keep, a_send, a_recv, b_send, b_recv, c_send, c_recv, d_send,
     send_sem, local_sem, row_sem, g_sem, a_sem, b_sem, c_sem, d_sem,
 ):
@@ -108,19 +109,27 @@
         target = jnp.where(expert == d, plan[d], target)
     expert = jnp.where((named & 1) == 0, expert, target)
     gate = gates[...]
+    grow_send[...] = jnp.zeros_like(grow_send)
     for e in range(experts):
-        column = jnp.sum(jnp.where(expert == e, gate, 0.0), axis=1, keepdims=True)
-        grow_send[e] = jnp.sum(jnp.where(diagonal, column, 0.0), axis=0, keepdims=True)
+        grow_send[e, :, :tok] = jnp.sum(jnp.where(expert == e, gate, 0.0), axis=0, keepdims=True)
 
     pl.semaphore_wait(barrier, experts)
 
-    for step in (1, -1):
-        send(
-            tokens.at[:, mine], rows.at[0, 0, z], row_sem.at[0, 0, z],
-            {"expert": (z + step) * 2 + c}, (z + step >= 0) & (z + step < nz),
-        )
-    send(tokens.at[:, mine], rows.at[0, 1, z], row_sem.at[0, 1, z], partner)
-    send(tokens.at[:, other], rows.at[1, 1, z], row_sem.at[1, 1, z], partner)
+    pieces = tok // ROWS
+    cuts = [pl.ds(q * ROWS, ROWS) for q in range(pieces)]
+
+    def piece(h, r, slot, q):
+        return rows.at[h, r, slot, cuts[q]], row_sem.at[h, r, slot, q]
+
+    for q in range(pieces):
+        for step in (1, -1):
+            send(
+                tokens.at[cuts[q], mine], *piece(0, 0, z, q),
+                {"expert": (z + step) * 2 + c}, (z + step >= 0) & (z + step < nz),
+            )
+    for h, part in enumerate((mine, other)):
+        for q in range(pieces):
+            send(tokens.at[cuts[q], part], *piece(h, 1, z, q), partner)
     for dz in range(nz):
         for r in range(2):
             if dz or r:
@@ -128,29 +137,64 @@
                 send(grow_send.at[peer], grow.at[r, z], g_sem.at[r, z], {"expert": peer})
     grow[0, z] = grow_send[me]
 
-    for hop in range(1, nz + 1):
+    items = [(hop, q) for hop in range(1, nz) for q in range(pieces)]
+
+    def from_z(hop, q):
         for step in (1, -1):
-            if hop < nz:
-                origin = z - step * hop
-                valid = (origin >= 0) & (origin < nz)
-                slot = jnp.clip(origin, 0, nz - 1)
-                block = rows.at[0, 0, slot]
-                pl.when(valid)(functools.partial(arrived, block, row_sem.at[0, 0, slot]))
-                if hop < nz - 1:
-                    send(
-                        block, block, row_sem.at[0, 0, slot], {"expert": (z + step) * 2 + c},
-                        valid & (z + step >= 0) & (z + step < nz),
-                    )
-                send(block, rows.at[1, 0, slot], row_sem.at[1, 0, slot], across, valid)
-                send(block, rows.at[0, 1, slot], row_sem.at[0, 1, slot], partner, valid)
+            origin = z - step * hop
+            valid = (origin >= 0) & (origin < nz)
+            slot = jnp.clip(origin, 0, nz - 1)
+            block, sem = piece(0, 0, slot, q)
+            pl.when(valid)(functools.partial(arrived, block, sem))
+            if hop < nz - 1:
+                send(
+                    block, block, sem, {"expert": (z + step) * 2 + c},
+                    valid & (z + step >= 0) & (z + step < nz),
+                )
+            send(block, *piece(1, 0, slot, q), across, valid)
+            send(block, *piece(0, 1, slot, q), partner, valid)
+
+    def from_across(hop, q):
         for step in (1, -1):
-            if hop > 1:
-                origin = z - step * (hop - 1)
-                valid = (origin >= 0) & (origin < nz)
-                slot = jnp.clip(origin, 0, nz - 1)
-                block = rows.at[1, 0, slot]
-                pl.when(valid)(functools.partial(arrived, block, row_sem.at[1, 0, slot]))
-                send(block, rows.at[1, 1, slot], row_sem.at[1, 1, slot], partner, valid)
+            origin = z - step * hop
+            valid = (origin >= 0) & (origin < nz)
+            slot = jnp.clip(origin, 0, nz - 1)
+            block, sem = piece(1, 0, slot, q)
+            pl.when(valid)(functools.partial(arrived, block, sem))
+            send(block, *piece(1, 1, slot, q), partner, valid)
+
+    def from_partner(h):
+        for dz in range(nz):
+            for q in range(pieces):
+                arrived(*piece(h, 1, (z + dz) % nz, q))
+
+    total = 2 * nz * tok
+    units = wg.shape[-1]
+    tile = 256 if units % 256 == 0 else LANES
+    tiles = [pl.ds(t * tile, tile) for t in range(units // tile)]
+
+    def product(h, weights, cols):
+        return jnp.dot(
+            rows[h].reshape(total, half), weights[h, :, cols], preferred_element_type=f32
+        )
+
+    late = 2
+    for i, item in enumerate(items):
+        from_z(*item)
+        if i >= late:
+            from_across(*items[i - late])
+
+    for copy in own_copies + weight_copies[:2]:
+        copy.wait()
+    from_partner(0)
+    rest = list(items[-late:])
+    for cols in tiles:
+        acc[0, :, cols] = product(0, wg, cols)
+        acc[1, :, cols] = product(0, wu, cols)
+        if rest:
+            from_across(*rest.pop(0))
+    for item in rest:
+        from_across(*item)
 
     for dz in range(nz):
         for r in range(2):
@@ -161,25 +205,12 @@
         for i in range(nz):
             column = jnp.sum(jnp.where(diagonal, grow[r, i], 0.0), axis=1, keepdims=True)
             scale[r, i] = jnp.broadcast_to(column, (tok, width))
-    for copy in own_copies + weight_copies:
+    for copy in weight_copies[2:]:
         copy.wait()
-    for dz in range(nz):
-        slot = (z + dz) % nz
-        for h in range(2):
-            arrived(rows.at[h, 1, slot], row_sem.at[h, 1, slot])
-
-    total = 2 * nz * tok
-    units = wg.shape[-1]
-    tile = 256 if units % 256 == 0 else LANES
-    for t in range(units // tile):
-        cols = pl.ds(t * tile, tile)
-        gate_act = up_act = None
-        for h in range(2):
-            block = rows[h].reshape(total, half)
-            g = jnp.dot(block, wg[h, :, cols], preferred_element_type=f32)
-            u = jnp.dot(block, wu[h, :, cols], preferred_element_type=f32)
-            gate_act = g if gate_act is None else gate_act + g
-            up_act = u if up_act is None else up_act + u
+    from_partner(1)
+    for cols in tiles:
+        gate_act = acc[0, :, cols] + product(1, wg, cols)
+        up_act = acc[1, :, cols] + product(1, wu, cols)
         hid[:, cols] = (gate_act / (1.0 + jnp.exp(-gate_act)) * up_act).astype(bf16)
 
     for copy in down_copies:
@@ -252,7 +283,7 @@
     steps = half // width
     dma = pltpu.SemaphoreType.DMA
     vmem, anywhere = pl.BlockSpec(memory_space=pltpu.VMEM), pl.BlockSpec(memory_space=pl.ANY)
-    sends = 4 + 2 * nz + 8 * nz + steps * (3 + nz) + 4
+    sends = 2 * nz + (4 + 8 * nz) * (tok // ROWS) + steps * (3 + nz)
     return pl.pallas_call(
         functools.partial(kernel, nz, steps, width),
         out_shape=jax.ShapeDtypeStruct((tok, model), bf16),
@@ -266,6 +297,7 @@
             pltpu.VMEM((2, half, units), bf16),
             pltpu.VMEM((2, half, units), bf16),
             pltpu.VMEM((2, half, units), bf16),
+            pltpu.VMEM((2, 2 * nz * tok, units), f32),
             pltpu.VMEM((2 * nz * tok, units), bf16),
             pltpu.VMEM((2, nz, tok, width), f32),
             pltpu.VMEM((2 * nz, 1, LANES), f32),
@@ -280,17 +312,15 @@
             pltpu.VMEM((steps, tok, width), bf16),
             dma((sends,)),
             dma((8 + steps,)),
-            dma((2, 2, nz)),
+            dma((2, 2, nz, tok // ROWS)),
             dma((2, nz)),
             dma((2, steps)),
             dma((steps,)),
             dma((steps, nz - 1)),
             dma((steps,)),
         ],
-        compiler_params=pltpu.CompilerParams(
-            collective_id=0, has_side_effects=True, vmem_limit_bytes=48 * 1024 * 1024
-        ),
-    )(tokens, gates, slots, plan, gate_proj, up_proj, down_proj)
+        compiler_params=pltpu.CompilerParams(collective_id=0, has_side_effects=True),
+    )(tokens, gates.T, slots.T, plan, gate_proj, up_proj, down_proj)
 
 
 def body(tokens, gates, slots, plan, gate_proj, up_proj, down_proj):
@@ -298,7 +328,7 @@
     tok, model = tokens.shape
     fits = (
         attn == 2 and experts % 2 == 0 and experts > 2
-        and tok % 16 == 0 and tok <= LANES
+        and tok % ROWS == 0 and tok <= LANES
         and model % (2 * LANES) == 0 and gate_proj.shape[0] == 1
         and gate_proj.shape[2] % LANES == 0
     )

time: 53.5 us -> 47.1 us (0.88)
  local copies, waits for them, and re-layouts: 5.84 us -> 1.64 us
  Pallas kernels: 47.4 us -> 45.3 us
    unnamed x9 -> x1, local copies, waits for them, and re-layouts: 5.84 us -> 1.64 us
    pallas_call x1, Pallas kernels: 47.4 us -> 45.3 us  [fused_body(): pl.pallas_call(functools.partial(kernel, nz, steps, width), out_shape=jax...]
where the time goes in v2:
time: 47.1 us; the launch traced here: 46.9 us
  Pallas kernels  45.3 us (96%)
  local copies, waits for them, and re-layouts  1.64 us (3%)
    pallas_call x1, Pallas kernels, fused_body(): pl.pallas_call(functools.partial(kernel, nz, steps, width), out_shape=jax...  45.3 us
    unnamed x1, local copies, waits for them, and re-layouts  1.64 us

profile of v2, /device:TPU:0, one launch (start us, length us, event | category | flops | bytes accessed | tf_op | source)
XLA Modules:
  0.0 46.9 jit_solution(15401195849400227209)
XLA Ops:
  0.0 45.3 %shard_map.73 = bf16[32,3584]{1,0:T(8,128)(2,1)} custom-call(bf16[32,3584]{1,0:T(8,128)(2,1)} %tokens.1, f32[8,32]{1,0:T(8,128)} %bitcast.2, s32[8,32]{1,0:T(8,128)} %bitcast.3, s32[8]{0:T(128)} %plan.1, bf16[1,3584,512]{2,1,0:T(8,128)(2,1)} %gate_hbm.1, bf16[1,3584,512]{2,1,0:T(8,128)(2,1)} %up_hbm.1, bf16[1,3584,512]{2,1,0:T(8,128)(2,1)} %down_hbm.1), custom_call_target="tpu_custom_call" | custom-call | tf_op jit(solution)/shard_map/pallas_call | solution.py:287
  45.3 1.6 %copy.9 = bf16[32,3584]{1,0:T(8,128)(2,1)} copy(bf16[32,3584]{1,0:T(8,128)(2,1)} %shard_map.73) | data formatting | bytes 458752

commit v3 on v2

--- a/solution.py
+++ b/solution.py
@@ -9,8 +9,9 @@
 
 MESH = pl.DeviceIdType.MESH
 LANES = 128
-LAG = 3
+LAG = 5
 ROWS = 16
+Z_FIRST = 2
 
 
 def combined_gates(gates, slots, plan, experts):
@@ -35,12 +36,13 @@
 
 
 def kernel(
-    nz, steps, width,
+    nz, steps, width, z_first,
     tokens, gates, slots, plan, gate_hbm, up_hbm, down_hbm,
     out,
     rows, wg, wu, wd, acc, hid, scale, grow_send, grow,
     keep, a_send, a_recv, b_send, b_recv, c_send, c_recv, d_send,
-    send_sem, local_sem, row_sem, g_sem, a_sem, b_sem, c_sem, d_sem,
+    zc_send, zc_recv, e_send, e_recv, e_out,
+    send_sem, local_sem, row_sem, g_sem, a_sem, b_sem, c_sem, d_sem, zc_sem, e_sem,
 ):
     f32, bf16 = jnp.float32, jnp.bfloat16
     experts = 2 * nz
@@ -221,19 +223,40 @@
         b_send[j] = (keep[1, j] + a_recv[1, j].astype(f32)).astype(bf16)
         send(b_send.at[j], b_recv.at[j], b_sem.at[j], across)
 
-    for j in range(steps):
-        for h in (1, 0):
-            down = lax.dot_general(
-                hid[...], wd[h, pl.ds(j * width, width), :], (((1,), (1,)), ((), ())),
-                preferred_element_type=f32,
-            )
-            down = down.reshape(2, nz, tok, width) * scale[...]
-            a_send[h, j] = down[1].astype(bf16)
-            keep[h, j] = down[0]
-            send(a_send.at[h, j], a_recv.at[h, j], a_sem.at[h, j], partner)
-        if j:
-            cross(j - 1)
-    cross(steps - 1)
+    early = steps - z_first
+    sums = [(h, j) for j in range(early, steps) for h in (1, 0)]
+
+    def along_z(h, j):
+        n = sums.index((h, j))
+        arrived(a_recv.at[h, j], a_sem.at[h, j])
+        zc_send[n] = (keep[h, j] + a_recv[h, j].astype(f32)).astype(bf16)
+        for d in range(nz - 1):
+            peer = (z + d + 1) % nz
+            send(zc_send.at[n, peer], zc_recv.at[n, d], zc_sem.at[n, d], {"expert": peer * 2 + c})
+
+    def after(h, j):
+        if j >= early:
+            along_z(h, j)
+        elif h:
+            cross(j)
+
+    order = [(1, j) for j in range(min(2, early))] + sums
+    for j in range(early):
+        if j + 2 < early:
+            order.append((1, j + 2))
+        order.append((0, j))
+    for i, (h, j) in enumerate(order):
+        down = lax.dot_general(
+            hid[...], wd[h, pl.ds(j * width, width), :], (((1,), (1,)), ((), ())),
+            preferred_element_type=f32,
+        )
+        down = down.reshape(2, nz, tok, width) * scale[...]
+        a_send[h, j] = down[1].astype(bf16)
+        keep[h, j] = down[0]
+        send(a_send.at[h, j], a_recv.at[h, j], a_sem.at[h, j], partner)
+        if i:
+            after(*order[i - 1])
+    after(*order[-1])
 
     out_copies = []
 
@@ -248,8 +271,25 @@
         send(d_send.at[j], out.at[:, cols], d_sem.at[j], across)
         out_copies.append(local(d_send.at[j], out.at[:, cols]))
 
-    for j in range(steps + LAG):
-        if j < steps:
+    def exchange(h, j):
+        n = sums.index((h, j))
+        value = keep[h, j, z] + a_recv[h, j, z].astype(f32)
+        for d in range(nz - 1):
+            arrived(zc_recv.at[n, d], zc_sem.at[n, d])
+        for d in range(nz - 1):
+            value = value + zc_recv[n, d].astype(f32)
+        e_send[n] = value.astype(bf16)
+        send(e_send.at[n], e_recv.at[n ^ 1], e_sem.at[n ^ 1], across)
+
+    def close(h, j):
+        n = sums.index((h, j))
+        arrived(e_recv.at[n], e_sem.at[n])
+        e_out[n] = (e_send[n].astype(f32) + e_recv[n].astype(f32)).astype(bf16)
+        start = (x if h == 0 else 1 - x) * half + j * width
+        out_copies.append(local(e_out.at[n], out.at[:, pl.ds(pl.multiple_of(start, LANES), width)]))
+
+    for j in range(early + LAG):
+        if j < early:
             arrived(a_recv.at[0, j], a_sem.at[0, j])
             arrived(b_recv.at[j], b_sem.at[j])
             c_send[j] = (keep[0, j] + a_recv[0, j].astype(f32) + b_recv[j].astype(f32)).astype(bf16)
@@ -258,10 +298,16 @@
                 send(
                     c_send.at[j, peer], c_recv.at[j, d], c_sem.at[j, d], {"expert": peer * 2 + c}
                 )
+        if j == min(z_first + 1, early - 1):
+            for pair in sums:
+                exchange(*pair)
         if j >= LAG:
             finish(j - LAG)
-
-    for j in range(steps):
+        if j == early:
+            for pair in sums:
+                close(*pair)
+
+    for j in range(early):
         cols = pl.ds(pl.multiple_of((1 - x) * half + j * width, LANES), width)
         arrived(out.at[:, cols], d_sem.at[j])
     for copy in out_copies:
@@ -281,11 +327,13 @@
     units = gate_proj.shape[2]
     width = 256 if half % 256 == 0 else LANES
     steps = half // width
+    z_first = min(Z_FIRST, steps - 1)
+    extra = max(1, 2 * z_first)
     dma = pltpu.SemaphoreType.DMA
     vmem, anywhere = pl.BlockSpec(memory_space=pltpu.VMEM), pl.BlockSpec(memory_space=pl.ANY)
-    sends = 2 * nz + (4 + 8 * nz) * (tok // ROWS) + steps * (3 + nz)
+    sends = extra * nz + 2 * nz + (4 + 8 * nz) * (tok // ROWS) + steps * (3 + nz)
     return pl.pallas_call(
-        functools.partial(kernel, nz, steps, width),
+        functools.partial(kernel, nz, steps, width, z_first),
         out_shape=jax.ShapeDtypeStruct((tok, model), bf16),
         in_specs=[
             anywhere, vmem, vmem, pl.BlockSpec(memory_space=pltpu.SMEM),
@@ -310,14 +358,21 @@
             pltpu.VMEM((steps, nz, tok, width), bf16),
             pltpu.VMEM((steps, nz - 1, tok, width), bf16),
             pltpu.VMEM((steps, tok, width), bf16),
+            pltpu.VMEM((extra, nz, tok, width), bf16),
+            pltpu.VMEM((extra, nz - 1, tok, width), bf16),
+            pltpu.VMEM((extra, tok, width), bf16),
+            pltpu.VMEM((extra, tok, width), bf16),
+            pltpu.VMEM((extra, tok, width), bf16),
             dma((sends,)),
-            dma((8 + steps,)),
+            dma((8 + steps + extra,)),
             dma((2, 2, nz, tok // ROWS)),
             dma((2, nz)),
             dma((2, steps)),
             dma((steps,)),
             dma((steps, nz - 1)),
             dma((steps,)),
+            dma((extra, nz - 1)),
+            dma((extra,)),
         ],
         compiler_params=pltpu.CompilerParams(collective_id=0, has_side_effects=True),
     )(tokens, gates.T, slots.T, plan, gate_proj, up_proj, down_proj)

time: 47.1 us -> 46.5 us (0.987)
  Pallas kernels: 45.3 us -> 44.7 us
    pallas_call x1, Pallas kernels: 45.3 us -> 44.7 us  [fused_body(): pl.pallas_call(functools.partial(kernel, nz, steps, width, z_first), out_...]
where the time goes in v3:
time: 46.5 us; the launch traced here: 46.3 us
  Pallas kernels  44.7 us (96%)
  local copies, waits for them, and re-layouts  1.64 us (4%)
    pallas_call x1, Pallas kernels, fused_body(): pl.pallas_call(functools.partial(kernel, nz, steps, width, z_first), out_...  44.7 us
    unnamed x1, local copies, waits for them, and re-layouts  1.64 us

profile of v3, /device:TPU:0, one launch (start us, length us, event | category | flops | bytes accessed | tf_op | source)
XLA Modules:
  0.0 46.3 jit_solution(11347959602602243832)
XLA Ops:
  0.0 44.7 %shard_map.73 = bf16[32,3584]{1,0:T(8,128)(2,1)} custom-call(bf16[32,3584]{1,0:T(8,128)(2,1)} %tokens.1, f32[8,32]{1,0:T(8,128)} %bitcast.2, s32[8,32]{1,0:T(8,128)} %bitcast.3, s32[8]{0:T(128)} %plan.1, bf16[1,3584,512]{2,1,0:T(8,128)(2,1)} %gate_hbm.1, bf16[1,3584,512]{2,1,0:T(8,128)(2,1)} %up_hbm.1, bf16[1,3584,512]{2,1,0:T(8,128)(2,1)} %down_hbm.1), custom_call_target="tpu_custom_call" | custom-call | tf_op jit(solution)/shard_map/pallas_call | solution.py:335
  44.7 1.6 %copy.9 = bf16[32,3584]{1,0:T(8,128)(2,1)} copy(bf16[32,3584]{1,0:T(8,128)(2,1)} %shard_map.73) | data formatting | bytes 458752

commit v4 on v3

--- a/solution.py
+++ b/solution.py
@@ -180,7 +180,7 @@
             rows[h].reshape(total, half), weights[h, :, cols], preferred_element_type=f32
         )
 
-    late = 2
+    late = 3
     for i, item in enumerate(items):
         from_z(*item)
         if i >= late:

time: 46.5 us -> 45.5 us (0.978)
  Pallas kernels: 44.7 us -> 43.7 us
    pallas_call x1, Pallas kernels: 44.7 us -> 43.7 us  [fused_body(): pl.pallas_call(functools.partial(kernel, nz, steps, width, z_first), out_...]
where the time goes in v4:
time: 45.5 us; the launch traced here: 45.4 us
  Pallas kernels  43.7 us (96%)
  local copies, waits for them, and re-layouts  1.64 us (4%)
    pallas_call x1, Pallas kernels, fused_body(): pl.pallas_call(functools.partial(kernel, nz, steps, width, z_first), out_...  43.7 us
    unnamed x1, local copies, waits for them, and re-layouts  1.64 us

profile of v4, /device:TPU:0, one launch (start us, length us, event | category | flops | bytes accessed | tf_op | source)
XLA Modules:
  0.0 45.4 jit_solution(5022333007156443895)
XLA Ops:
  0.0 43.7 %shard_map.73 = bf16[32,3584]{1,0:T(8,128)(2,1)} custom-call(bf16[32,3584]{1,0:T(8,128)(2,1)} %tokens.1, f32[8,32]{1,0:T(8,128)} %bitcast.2, s32[8,32]{1,0:T(8,128)} %bitcast.3, s32[8]{0:T(128)} %plan.1, bf16[1,3584,512]{2,1,0:T(8,128)(2,1)} %gate_hbm.1, bf16[1,3584,512]{2,1,0:T(8,128)(2,1)} %up_hbm.1, bf16[1,3584,512]{2,1,0:T(8,128)(2,1)} %down_hbm.1), custom_call_target="tpu_custom_call" | custom-call | tf_op jit(solution)/shard_map/pallas_call | solution.py:335
  43.7 1.6 %copy.9 = bf16[32,3584]{1,0:T(8,128)(2,1)} copy(bf16[32,3584]{1,0:T(8,128)(2,1)} %shard_map.73) | data formatting | bytes 458752
